TPU v7x, 256 devices: a whole 4x4x8 slice. The times are simulated.
256 devices in a mesh: mode: 8 (over x, core), body: 32 (over y, z).
Axes of the slice: x: 4, y: 4, z: 8, core: 2. Of those that a mesh axis runs over, the one named last changes fastest.
Arguments:
- incident: bfloat16 [32, 32, 2, 8, 512], P('body', 'mode'), may hold values from -6 to 6
- inverse: bfloat16 [32, 32, 2, 512, 512], P('body', 'mode'), may hold values from -0.1875 to 0.1875
- coupling: bfloat16 [32, 2, 512, 384], P('body'), may hold values from -0.21875 to 0.21875
- cycle_weight: bfloat16 [32, 256, 384], P('body', 'mode'), may hold values from 0.5 to 4
- near_bodies: int32 [32, 6], replicated, may hold values from 0 to 31, as said below
- cycle_nodes: int32 [32, 6, 64], replicated, may hold values from 0 to 511
- cycle_counts: int32 [32, 6], replicated, may hold values from 1 to 64, as said below
Outputs:
- density: bfloat16 [32, 32, 2, 8, 512], P('body', 'mode')
Inputs may be any that keep to these rules, and one draw needn't show every extreme that they name: `near_bodies`: each row lists 6 different bodies, none equal to the row's own index. `cycle_nodes`: entries past a slot's live count are drawn as well and are not used. Only the first cycle_counts[t, n] entries of cycle_nodes[t, n] are live; in every draw some entry of cycle_counts equals 64.
All inputs are finite; a program needn't handle non-finite values.
Results may differ from a plain program's by a relative error of at most 0.022.
Values may be sent and summed in bfloat16 or wider, within the bound.
A program may use at most 128 MiB of HBM per device.

v0:
```python
import math

import jax
import jax.numpy as jnp
from jax import lax
from jax.sharding import PartitionSpec as P

MODES = 32
NA = 256
ITERS = 2


def wave_values(count_modes, first_angle, count_angles):
    wavenum = jnp.arange(count_modes, dtype=jnp.int32) - MODES // 2
    angle_index = first_angle + jnp.arange(count_angles, dtype=jnp.int32)
    residue = wavenum[:, None] * angle_index[None, :] % NA
    theta_values = residue.astype(jnp.float32) * (2.0 * math.pi / NA)
    return (jnp.cos(theta_values), jnp.sin(theta_values))


def upward_table(cosine_part, sine_part):
    return jnp.stack(
        [jnp.stack([cosine_part, sine_part], -1), jnp.stack([-sine_part, cosine_part], -1)], 1
    ).astype(jnp.bfloat16)


def downward_table(cosine_part, sine_part):
    flip_cos = cosine_part.T
    flip_sin = sine_part.T
    return jnp.stack(
        [jnp.stack([flip_cos, -flip_sin], -1), jnp.stack([flip_sin, flip_cos], -1)], 1
    ).astype(jnp.bfloat16)


def apply_inverse(inverse_blocks, right_side):
    product = jnp.einsum(
        "mcqp,mdip->mcdiq", inverse_blocks, right_side, preferred_element_type=jnp.float32
    )
    real_part = product[:, 0, 0] - product[:, 1, 1]
    imag_part = product[:, 1, 0] + product[:, 0, 1]
    return jnp.stack([real_part, imag_part], 1).astype(jnp.bfloat16)


def local(incident, inverse, coupling, cycle_weight, near_bodies, cycle_nodes, cycle_counts):
    mode_index = lax.axis_index("mode")
    body_index = lax.axis_index("body")
    incidences = incident.shape[3]
    sector = cycle_weight.shape[1]
    bodies_all = near_bodies.shape[0]
    neighbours = near_bodies.shape[1]
    capacity = cycle_nodes.shape[2]
    slot_count = neighbours * capacity
    cosine_part, sine_part = wave_values(MODES, mode_index * sector, sector)
    upward = upward_table(cosine_part, sine_part)
    downward = downward_table(cosine_part, sine_part)
    downward_wide = downward.astype(jnp.float32)
    own_list = lax.dynamic_index_in_dim(near_bodies, body_index, 0, keepdims=False)
    listed = near_bodies == body_index
    send_nodes = jnp.sum(jnp.where(listed[:, :, None], cycle_nodes, 0), axis=1)
    send_counts = jnp.sum(jnp.where(listed, cycle_counts, 0), axis=1)
    send_live = jnp.arange(capacity, dtype=jnp.int32)[None, :] < send_counts[:, None]
    weights = cycle_weight[0].T.astype(jnp.float32)
    density = apply_inverse(inverse[0], incident[0])
    for iteration in range(ITERS):
        all_density = lax.all_gather(density, "mode", axis=0, tiled=True)
        upsampled = jnp.einsum(
            "kcip,kcad->padi", all_density, upward, preferred_element_type=jnp.float32
        ).astype(jnp.bfloat16)
        flat_cycles = upsampled.reshape(upsampled.shape[0], -1)
        outgoing = jnp.where(send_live[:, :, None], flat_cycles[send_nodes], 0)
        incoming = lax.all_to_all(
            outgoing.reshape(bodies_all, -1), "body", split_axis=0, concat_axis=0, tiled=True
        )
        cycle_values = jnp.take(incoming, own_list, axis=0).reshape(
            slot_count, sector, 2, incidences
        )
        scaled = (cycle_values.astype(jnp.float32) * weights[:, :, None, None]).astype(jnp.bfloat16)
        stacked = scaled.reshape(slot_count, -1)
        real_rows = jnp.dot(coupling[0, 0], stacked, preferred_element_type=jnp.float32).reshape(
            -1, sector, 2, incidences
        )
        imag_rows = jnp.dot(coupling[0, 1], stacked, preferred_element_type=jnp.float32).reshape(
            -1, sector, 2, incidences
        )
        near_field = jnp.stack(
            [real_rows[:, :, 0] - imag_rows[:, :, 1], imag_rows[:, :, 0] + real_rows[:, :, 1]], 2
        )
        correction = lax.psum_scatter(
            jnp.einsum(
                "qadi,adkc->kciq", near_field, downward_wide, precision=lax.Precision.HIGHEST
            ).astype(jnp.bfloat16),
            "mode",
            scatter_dimension=0,
            tiled=True,
        ).astype(jnp.float32)
        residual_side = (incident[0].astype(jnp.float32) - correction * (1.0 / NA)).astype(
            jnp.bfloat16
        )
        density = apply_inverse(inverse[0], residual_side)
    return density[None]


def solution(mesh):
    in_specs = (
        P("body", "mode", None, None, None),
        P("body", "mode", None, None, None),
        P("body", None, None, None),
        P("body", "mode", None),
        P(),
        P(),
        P(),
    )
    out_specs = P("body", "mode", None, None, None)
    return jax.shard_map(local, mesh=mesh, in_specs=in_specs, out_specs=out_specs, check_vma=False)
```

profile of v0, /device:TPU:1, one launch (start us, length us, event | category | flops | bytes accessed | tf_op | source)
XLA Modules:
  0.0 446.6 jit_solution(414187136423698979)
XLA Ops:
  6.5 3.4 fusion.14
  10.1 16.1 %all_gather.6 = bf16[32,2,8,512]{3,2,0,1:T(8,128)(2,1)S(1)} all-gather(bf16[4,2,8,512]{3,2,0,1:T(8,128)(2,1)S(1)} %pad_maximum_fusion), channel_id=1, replica_groups=mesh['mode'=8,'body'=32] {'mode'}, dimensions={0}, use_global_device_ids=true | all-gather | bytes 589824 | tf_op jit(solution)/shard_map/all_gather | solution.py:65
  26.2 0.2 negate_convert_fusion.1
  26.5 0.3 fusion.11
  26.8 0.3 copy.104
  27.1 0.2 copy.105
  27.4 0.1 select_reduce_fusion
  27.5 0.1 reshape.696
  27.6 0.1 iota_compare_fusion
  27.6 9.2 %gather_fusion = bf16[2048,512]{1,0:T(8,128)(2,1)} fusion(bf16[512,512]{1,0:T(8,128)(2,1)S(1)} %copy.105, s32[2048]{0:T(1024)S(1)} %broadcast_clamp_fusion), kind=kCustom, calls=%fused_computation.2 | custom fusion | bytes 4202496 | tf_op jit(solution)/shard_map/gather | solution.py:70
  36.8 1.8 broadcast_select_fusion.1
  38.6 6.3 %select_n.116 = bf16[32,1,32768]{2,1,0:T(2,128)(2,1)} reshape(bf16[32,64,512]{2,1,0:T(8,128)(2,1)S(1)} %broadcast_select_fusion.1) | data formatting | bytes 4194304 | tf_op jit(solution)/shard_map/jit(_where)/select_n | solution.py:70
  44.9 0.5 broadcast.549
  45.4 13.2 %reduce.2 = bf16[32,32768]{1,0:T(8,128)(2,1)S(1)} reduce(bf16[32,1,32768]{2,1,0:T(2,128)(2,1)} %select_n.116, bf16[]{:T(256)} %broadcast.549), dimensions={1}, to_apply=%select_n.116.reduce_sub_computation | reduce | bytes 4194306 | tf_op jit(solution)/shard_map/jit(_where)/select_n | solution.py:70
  58.6 2.8 reshape.734
  61.3 9.9 %all-to-all-start = ((bf16[32,2,16384]{2,1,0:T(2,128)(2,1)}), bf16[32,2,16384]{2,1,0:T(2,128)(2,1)S(1)}, u32[]{:S(2)}, u32[]{:S(2)}) async-start(bf16[32,2,16384]{2,1,0:T(2,128)(2,1)} %reshape.734), calls=%async_computation | async-start | bytes 4194304 | tf_op jit(solution)/shard_map/all_to_all | solution.py:71
  71.3 0.2 dynamic-slice_reduce_fusion
  71.5 0.1 copy.107
  71.7 48.4 %all-to-all-done = bf16[32,2,16384]{2,1,0:T(2,128)(2,1)S(1)} async-done(((bf16[32,2,16384]{2,1,0:T(2,128)(2,1)}), bf16[32,2,16384]{2,1,0:T(2,128)(2,1)S(1)}, u32[]{:S(2)}, u32[]{:S(2)}) %all-to-all-start) | async-done | bytes 2097184 | tf_op jit(solution)/shard_map/all_to_all | solution.py:71
  120.1 6.9 %reshape.735 = bf16[32,1,32768]{2,1,0:T(2,128)(2,1)} reshape(bf16[32,2,16384]{2,1,0:T(2,128)(2,1)S(1)} %all-to-all-done) | data formatting | bytes 4194304
  127.0 4.5 %copy.185 = bf16[32,1,32768]{2,0,1:T(8,128)(2,1)S(1)} copy(bf16[32,1,32768]{2,1,0:T(2,128)(2,1)} %reshape.735) | data formatting | bytes 4194304
  131.5 0.8 gather_fusion.2
  132.3 0.1 select_convert_fusion.1
  132.5 24.6 %reshape.675 = f32[384,32,2,8]{3,2,1,0:T(2,128)} reshape(f32[6,32768]{1,0:T(8,128)S(1)} %select_convert_fusion.1) | data formatting | bytes 1572864 | tf_op jit(solution)/shard_map/convert_element_type | solution.py:77
  157.1 17.9 %multiply_convert_fusion.1 = bf16[384,32,2,8]{3,2,1,0:T(2,128)(2,1)} fusion(f32[384,32,2,8]{3,2,1,0:T(2,128)} %reshape.675, f32[384,32]{1,0:T(8,128)S(1)} %copy.107), kind=kLoop, calls=%fused_computation.5 | loop fusion | flops 393216 | bytes 1228800 | tf_op jit(solution)/shard_map/convert_element_type | solution.py:77
  175.0 12.8 %copy.108 = bf16[384,32,2,8]{0,3,2,1:T(8,128)(2,1)S(1)} copy(bf16[384,32,2,8]{3,2,1,0:T(2,128)(2,1)} %multiply_convert_fusion.1) | data formatting | bytes 786432 | tf_op jit(solution)/shard_map/convert_element_type | solution.py:77
  187.9 0.5 fusion.37
  188.4 0.5 fusion.33
  188.8 0.1 fusion.89
  188.9 0.1 fusion.90
  189.0 0.6 copy_subtract_fusion.1
  189.6 0.6 copy_add_fusion.1
  190.2 0.7 fusion.13
  190.9 1.1 copy.114
  192.0 30.5 %reduce-scatter.3.cloned.1.call-done = bf16[4,2,8,512]{3,2,1,0:T(8,128)(2,1)} async-done(((bf16[32,2,8,512]{3,2,1,0:T(8,128)(2,1)}), bf16[4,2,8,512]{3,2,1,0:T(8,128)(2,1)}) %reduce-scatter.3.cloned.1.call-update) | async-done | bytes 65552 | tf_op jit(solution)/shard_map/reduce_scatter | solution.py:88
  222.5 3.4 fusion.17
  226.0 15.8 %all_gather.7 = bf16[32,2,8,512]{3,2,0,1:T(8,128)(2,1)S(1)} all-gather(bf16[4,2,8,512]{3,2,0,1:T(8,128)(2,1)S(1)} %pad_maximum_fusion.1), channel_id=1, replica_groups=mesh['mode'=8,'body'=32] {'mode'}, dimensions={0}, use_global_device_ids=true | all-gather | bytes 589824 | tf_op jit(solution)/shard_map/all_gather | solution.py:65
  241.7 0.3 fusion.10
  242.1 0.3 copy.118
  242.4 0.2 copy.119
  242.6 9.2 %gather_fusion.1 = bf16[2048,512]{1,0:T(8,128)(2,1)} fusion(bf16[512,512]{1,0:T(8,128)(2,1)S(1)} %copy.119, s32[2048]{0:T(1024)S(1)} %broadcast_clamp_fusion), kind=kCustom, calls=%fused_computation.3 | custom fusion | bytes 4202496 | tf_op jit(solution)/shard_map/gather | solution.py:70
  251.8 1.8 broadcast_select_fusion
  253.6 6.3 %select_n.117 = bf16[32,1,32768]{2,1,0:T(2,128)(2,1)} reshape(bf16[32,64,512]{2,1,0:T(8,128)(2,1)S(1)} %broadcast_select_fusion) | data formatting | bytes 4194304 | tf_op jit(solution)/shard_map/jit(_where)/select_n | solution.py:70
  259.9 13.2 %reduce.3 = bf16[32,32768]{1,0:T(8,128)(2,1)S(1)} reduce(bf16[32,1,32768]{2,1,0:T(2,128)(2,1)} %select_n.117, bf16[]{:T(256)} %broadcast.549), dimensions={1}, to_apply=%select_n.117.reduce_sub_computation | reduce | bytes 4194306 | tf_op jit(solution)/shard_map/jit(_where)/select_n | solution.py:70
  273.0 2.8 reshape.736
  275.8 57.3 %all_to_all.18 = bf16[32,2,16384]{2,1,0:T(2,128)(2,1)S(1)} all-to-all(bf16[32,2,16384]{2,1,0:T(2,128)(2,1)} %reshape.736), channel_id=1, replica_groups=mesh['mode'=8,'body'=32] {'body'}, dimensions={0} | all-to-all | bytes 4194304 | tf_op jit(solution)/shard_map/all_to_all | solution.py:71
  333.1 7.1 %reshape.737 = bf16[32,1,32768]{2,1,0:T(2,128)(2,1)} reshape(bf16[32,2,16384]{2,1,0:T(2,128)(2,1)S(1)} %all_to_all.18) | data formatting | bytes 4194304
  340.2 4.5 %copy.184 = bf16[32,1,32768]{2,0,1:T(8,128)(2,1)S(1)} copy(bf16[32,1,32768]{2,1,0:T(2,128)(2,1)} %reshape.737) | data formatting | bytes 4194304
  344.7 0.8 gather_fusion.3
  345.5 0.1 select_convert_fusion
  345.7 24.6 %reshape.676 = f32[384,32,2,8]{3,2,1,0:T(2,128)} reshape(f32[6,32768]{1,0:T(8,128)S(1)} %select_convert_fusion) | data formatting | bytes 1572864 | tf_op jit(solution)/shard_map/convert_element_type | solution.py:77
  370.3 17.9 %multiply_convert_fusion = bf16[384,32,2,8]{3,2,1,0:T(2,128)(2,1)} fusion(f32[384,32,2,8]{3,2,1,0:T(2,128)} %reshape.676, f32[384,32]{1,0:T(8,128)S(1)} %copy-done.2), kind=kLoop, calls=%fused_computation.4 | loop fusion | flops 393216 | bytes 1228800 | tf_op jit(solution)/shard_map/convert_element_type | solution.py:77
  388.2 12.8 %copy.121 = bf16[384,32,2,8]{0,3,2,1:T(8,128)(2,1)S(1)} copy(bf16[384,32,2,8]{3,2,1,0:T(2,128)(2,1)} %multiply_convert_fusion) | data formatting | bytes 786432 | tf_op jit(solution)/shard_map/convert_element_type | solution.py:77
  401.0 0.5 fusion.31
  401.5 0.5 fusion.35
  401.9 0.1 fusion.88
  402.0 0.1 fusion.87
  402.1 0.6 copy_subtract_fusion
  402.7 0.6 copy_add_fusion
  403.3 0.7 fusion.12
  403.9 1.1 copy.127
  405.1 30.4 %reduce-scatter.5.cloned.1.call-done = bf16[4,2,8,512]{3,2,1,0:T(8,128)(2,1)} async-done(((bf16[32,2,8,512]{3,2,1,0:T(8,128)(2,1)}), bf16[4,2,8,512]{3,2,1,0:T(8,128)(2,1)}) %reduce-scatter.5.cloned.1.call-update) | async-done | bytes 65552 | tf_op jit(solution)/shard_map/reduce_scatter | solution.py:88
  435.5 3.4 fusion.20
  439.0 0.6 copy.130
  (39 shorter events, 0.4 us)
Async XLA Ops:
  6.5 20.8 %copy-start.6 = (s32[32,6]{0,1:T(8,128)S(1)}, s32[32,6]{0,1:T(8,128)}, u32[]{:S(2)}) copy-start(s32[32,6]{0,1:T(8,128)} %param.13) | copy-start | bytes 2308
  6.5 20.8 %copy-start.7 = (s32[32,6]{0,1:T(8,128)S(1)}, s32[32,6]{0,1:T(8,128)}, u32[]{:S(2)}) copy-start(s32[32,6]{0,1:T(8,128)} %param.15) | copy-start | bytes 2308
  6.5 20.8 %copy-start.4 = (s32[32,6,64]{2,0,1:T(8,128)S(1)}, s32[32,6,64]{2,0,1:T(8,128)}, u32[]{:S(2)}) copy-start(s32[32,6,64]{2,0,1:T(8,128)} %param.14) | copy-start | bytes 147460
  58.6 12.9 %copy-start.5 = (bf16[1,32,384]{2,1,0:T(8,128)(2,1)S(1)}, bf16[1,32,384]{2,1,0:T(8,128)(2,1)}, u32[]{:S(2)}) copy-start(bf16[1,32,384]{2,1,0:T(8,128)(2,1)} %param.12) | copy-start | bytes 73732
  61.3 58.8 %all-to-all-start = ((bf16[32,2,16384]{2,1,0:T(2,128)(2,1)}), bf16[32,2,16384]{2,1,0:T(2,128)(2,1)S(1)}, u32[]{:S(2)}, u32[]{:S(2)}) async-start(bf16[32,2,16384]{2,1,0:T(2,128)(2,1)} %reshape.734), calls=%async_computation | async-start | bytes 4194304 | tf_op jit(solution)/shard_map/all_to_all | solution.py:71
  71.2 151.3 %reduce-scatter.3.cloned.1.call-start = ((), (), s32[]{:S(2)}) async-start(), calls=%async_computation.4 | async-start | bytes 589824 | tf_op jit(solution)/shard_map/reduce_scatter | solution.py:88
  71.6 85.5 %copy-start.1 = (f32[384,32]{1,0:T(8,128)}, f32[384,32]{1,0:T(8,128)S(1)}, u32[]{:S(2)}) copy-start(f32[384,32]{1,0:T(8,128)S(1)} %copy.107) | copy-start | bytes 147460
  175.0 12.9 %copy-start = (bf16[1,2,512,384]{3,2,1,0:T(8,128)(2,1)S(1)}, bf16[1,2,512,384]{3,2,1,0:T(8,128)(2,1)}, u32[]{:S(2)}) copy-start(bf16[1,2,512,384]{3,2,1,0:T(8,128)(2,1)} %param.11) | copy-start | bytes 2359300
  188.9 33.5 %copy-start.3 = (bf16[1,4,2,8,512]{4,3,2,1,0:T(8,128)(2,1)S(1)}, bf16[1,4,2,8,512]{4,3,2,1,0:T(8,128)(2,1)}, u32[]{:S(2)}) copy-start(bf16[1,4,2,8,512]{4,3,2,1,0:T(8,128)(2,1)} %param.9) | copy-start | bytes 196612
  192.0 243.5 %reduce-scatter.5.cloned.1.call-start = ((), (), s32[]{:S(2)}) async-start(), calls=%async_computation.5 | async-start | bytes 589824 | tf_op jit(solution)/shard_map/reduce_scatter | solution.py:88
  345.7 24.6 %copy-start.2 = (f32[384,32]{1,0:T(8,128)S(1)}, f32[384,32]{1,0:T(8,128)}, u32[]{:S(2)}) copy-start(f32[384,32]{1,0:T(8,128)} %copy-done.1) | copy-start | bytes 147460
Sparse Core Ops, SparseCore 0:
  192.1 30.3 reduce-scatter.2
  405.2 30.2 reduce-scatter.4
where the time goes:
time: 454 us; the launch traced here: 447 us
  local copies, waits for them, and re-layouts  141 us (31%)
  waiting for transfers between devices  109 us (24%)
  blocking collectives  89.2 us (20%)
  other arithmetic  68.9 us (15%)
  matrix products  14.1 us (3%)
  between operations  14 us (3%)
  starting transfers between devices  9.94 us (2%)
    reduce_scatter x2, waiting for transfers between devices, local(): lax.psum_scatter(jnp.einsum('qadi,adkc->kciq', near_field, downward_wide,...  60.9 us
    all_to_all x1, blocking collectives, local(): lax.all_to_all(outgoing.reshape(bodies_all, -1), 'body', split_axis=0, co...  57.3 us
    convert_element_type x2, local copies, waits for them, and re-layouts, local(): cycle_values.astype(jnp.float32) * weights[:, :, None, None]  49.2 us
    all_to_all x1, waiting for transfers between devices, local(): lax.all_to_all(outgoing.reshape(bodies_all, -1), 'body', split_axis=0, co...  48.4 us
    convert_element_type x2, other arithmetic, local(): (cycle_values.astype(jnp.float32) * weights[:, :, None, None]).astype(jnp...  35.9 us
    all_gather x2, blocking collectives, local(): all_density = lax.all_gather(density, 'mode', axis=0, tiled=True)  31.9 us
    select_n x5, other arithmetic, local(): outgoing = jnp.where(send_live[:, :, None], flat_cycles[send_nodes], 0)  29.8 us
    unnamed x22, local copies, waits for them, and re-layouts  28.6 us
  transfers between devices with their start and end apart: 3, of which 3 were waited for; matrix products, arithmetic and copies ran while one was open for 0% of the time, Pallas kernels for 0%

commit v1 on v0

v1 whole, which is shorter than its diff:
```python
import math

import jax
import jax.numpy as jnp
import numpy as np
from jax import lax
from jax.experimental import pallas as pl
from jax.experimental.pallas import tpu as pltpu
from jax.sharding import PartitionSpec as P

MODES = 32
NA = 256
ITERS = 2
ZDIM = 8
MESH = pl.DeviceIdType.MESH
BF = jnp.bfloat16
F32 = jnp.float32


def tables():
    wavenum = np.arange(MODES) - MODES // 2
    residue = (wavenum[:, None] * np.arange(NA)[None, :]) % NA
    theta = residue.astype(np.float32) * np.float32(2.0 * math.pi / NA)
    cos, sin = np.cos(theta), np.sin(theta)
    up = np.stack([np.stack([cos, sin], -1), np.stack([-sin, cos], -1)], 1)
    up = up.transpose(3, 2, 0, 1).reshape(2 * NA, 2 * MODES)
    down = np.stack([np.stack([cos, sin], 1), np.stack([-sin, cos], 1)], 1)
    turned = np.stack([-down[:, 1], down[:, 0]], 1)
    down = np.concatenate([down.reshape(2 * MODES, 2 * NA), turned.reshape(2 * MODES, 2 * NA)], 0)
    return up.astype(BF), down.astype(BF)


def offsets(bodies):
    ydim = bodies // ZDIM
    far = lambda d, n: min(d, n - d)
    order = [(dy, dz) for dy in range(ydim) for dz in range(ZDIM)]
    order.sort(key=lambda o: (-far(o[1], ZDIM), -far(o[0], ydim), o))
    return order


def target(body, dy, dz, ydim):
    return lax.rem(body // ZDIM + dy, ydim) * ZDIM + lax.rem(lax.rem(body, ZDIM) + dz, ZDIM)


def dot_nt(left, right):
    return lax.dot_general(left, right, (((1,), (1,)), ((), ())), preferred_element_type=F32)


def kernel(
    n_mode, n_body, near_ref, nodes_ref, up_ref, down_ref, inc_ref, w_ref, inv_hbm, coup_hbm, out_ref,
    inv_v, coup_v, onehot, dens, snd1, recv1a, recv1b, gbuf, snd2, recv2, snd3, recv3, rbuf, wall,
    load_sem, send_sem, recv_sem,
):
    me = lax.axis_index("mode")
    body = lax.axis_index("body")
    ydim = n_body // ZDIM
    modes = inv_v.shape[0]
    near = near_ref.shape[1]
    cap = 64
    tiles = rbuf.shape[0]

    loads = [pltpu.make_async_copy(inv_hbm.at[k], inv_v.at[k], load_sem.at[k]) for k in range(modes)]
    loads.append(pltpu.make_async_copy(coup_hbm, coup_v, load_sem.at[modes]))
    for load in loads:
        load.start()

    barrier = pltpu.get_barrier_semaphore()

    @pl.loop(1, n_body)
    def _(off):
        pl.semaphore_signal(
            barrier, inc=1, device_id={"body": lax.rem(body + off, n_body)}, device_id_type=MESH
        )

    @pl.loop(1, n_mode)
    def _(off):
        pl.semaphore_signal(
            barrier, inc=1, device_id={"mode": lax.rem(me + off, n_mode)}, device_id_type=MESH
        )

    groups = onehot.shape[0]
    width = onehot.shape[2]
    node_index = lax.broadcasted_iota(jnp.int32, onehot.shape[1:], 0)
    for g in range(groups):
        row = nodes_ref[:, g * width : (g + 1) * width]
        onehot[g] = jnp.where(node_index == row, 1.0, 0.0).astype(BF)

    def to_modes(src, dst, slot):
        @pl.loop(1, n_mode)
        def _(off):
            peer = lax.rem(me + off, n_mode)
            pltpu.make_async_remote_copy(
                src_ref=src.at[peer], dst_ref=dst.at[me], send_sem=send_sem.at[slot],
                recv_sem=recv_sem.at[slot], device_id={"mode": peer}, device_id_type=MESH,
            ).start()

        pltpu.make_async_copy(src.at[me], dst.at[me], recv_sem.at[slot]).start()

    def arrived(dst, slot):
        pltpu.make_async_copy(dst, dst, recv_sem.at[slot]).wait()

    def sent(src, slot, count):
        part = src.at[pl.ds(0, count)]
        pltpu.make_async_copy(part, part, send_sem.at[slot]).wait()

    lane = lax.broadcasted_iota(jnp.int32, (32, 128), 1)
    low = lane < cap

    def inverse_product(k, real, imag):
        first = jnp.concatenate([real, imag], 0).astype(BF)
        second = jnp.concatenate([-imag, real], 0).astype(BF)
        return dot_nt(first, inv_v[k, 0]) + dot_nt(second, inv_v[k, 1])

    for k in range(modes):
        loads[k].wait()
        value = inverse_product(k, inc_ref[k, 0].astype(F32), inc_ref[k, 1].astype(F32))
        dens[16 * k : 16 * k + 16] = value.astype(BF)

    pl.semaphore_wait(barrier, n_body + n_mode - 2)

    @pl.loop(1, n_mode)
    def _(off):
        pltpu.make_async_remote_copy(
            src_ref=w_ref, dst_ref=wall.at[me], send_sem=send_sem.at[6], recv_sem=recv_sem.at[6],
            device_id={"mode": lax.rem(me + off, n_mode)}, device_id_type=MESH,
        ).start()

    pltpu.make_async_copy(w_ref, wall.at[me], recv_sem.at[6]).start()

    order = offsets(n_body)
    per_group = width // cap
    for it in range(ITERS):
        to_body, from_body = snd1.at[it], (recv1a, recv1b)[it]

        def send_group(g, it=it, to_body=to_body, from_body=from_body):
            for r in range(g * per_group, (g + 1) * per_group):
                if r == n_body - 1:
                    pltpu.make_async_copy(to_body.at[r], from_body.at[body], recv_sem.at[3 * it]).start()
                else:
                    pltpu.make_async_remote_copy(
                        src_ref=to_body.at[r], dst_ref=from_body.at[body], send_sem=send_sem.at[3 * it],
                        recv_sem=recv_sem.at[3 * it],
                        device_id={"body": target(body, *order[r], ydim)}, device_id_type=MESH,
                    ).start()

        all_dens = dens[...]
        for g in range(groups):
            picked = jnp.dot(all_dens, onehot[g], preferred_element_type=F32)
            for pair in range(per_group // 2):
                part = picked[:, 128 * pair : 128 * pair + 128]
                top, bottom = part[:32], part[32:]
                r = g * per_group + 2 * pair
                snd1[it, r] = jnp.where(low, top, pltpu.roll(bottom, cap, 1)).astype(BF)
                snd1[it, r + 1] = jnp.where(low, pltpu.roll(top, cap, 1), bottom).astype(BF)
            if g > 0:
                send_group(g - 1)
        send_group(groups - 1)

        arrived(from_body, 3 * it)
        for v in range(near // 2):
            a = from_body[near_ref[body, 2 * v]].astype(F32)
            b = from_body[near_ref[body, 2 * v + 1]].astype(F32)
            gbuf[v, 0:32] = jnp.where(low, a, pltpu.roll(b, cap, 1))
            gbuf[v, 32:64] = jnp.where(low, pltpu.roll(a, cap, 1), b)
        for i in range(n_mode):
            picked = [gbuf[v, pl.ds(i, 8, stride=8), :] for v in range(near // 2)]
            snd2[it, i] = jnp.concatenate(picked, 1).astype(BF)
        to_modes(snd2.at[it], recv2.at[it], 3 * it + 1)
        arrived(recv2.at[it], 3 * it + 1)

        modal = jnp.concatenate([recv2[it, j].astype(F32) for j in range(n_mode)], 0).astype(BF)
        cycles = jnp.dot(up_ref[...], modal, preferred_element_type=F32)
        if it == 0:
            arrived(wall, 6)
            loads[modes].wait()
        weights = wall[...].astype(F32).reshape(NA, -1)
        scaled = jnp.concatenate([cycles[:NA] * weights, cycles[NA:] * weights], 0).astype(BF)
        back = jnp.dot(down_ref[...], scaled, preferred_element_type=F32).astype(BF)
        half = back.shape[0] // 2
        correction = dot_nt(back[:half], coup_v[0]) + dot_nt(back[half:], coup_v[1])
        for j in range(n_mode):
            snd3[it, j] = correction[8 * j : 8 * j + 8].astype(BF)
        to_modes(snd3.at[it], recv3.at[it], 3 * it + 2)
        arrived(recv3.at[it], 3 * it + 2)

        for i in range(n_mode):
            value = recv3[it, i].astype(F32)
            for q in range(tiles):
                rbuf[q, 8 * i : 8 * i + 8] = value[:, 128 * q : 128 * q + 128]
        for k in range(modes):
            sides = []
            for c in range(2):
                value = [rbuf[q, pl.ds(2 * k + c, 8, stride=8), :] for q in range(tiles)]
                value = jnp.concatenate(value, 1)
                sides.append(inc_ref[k, c].astype(F32) - value * (1.0 / NA))
            value = inverse_product(k, *sides).astype(BF)
            if it < ITERS - 1:
                dens[16 * k : 16 * k + 16] = value
            else:
                out_ref[16 * k : 16 * k + 16] = value

    for it in range(ITERS):
        sent(snd1.at[it], 3 * it, n_body - 1)
        sent(snd2.at[it], 3 * it + 1, n_mode - 1)
        sent(snd3.at[it], 3 * it + 2, n_mode - 1)
    sent(wall, 6, n_mode - 1)


def solution(mesh):
    n_mode, n_body = mesh.shape["mode"], mesh.shape["body"]
    up, down = tables()
    dy, dz = (np.array(x, np.int32) for x in zip(*offsets(n_body)))

    def local(incident, inverse, coupling, cycle_weight, near_bodies, cycle_nodes, cycle_counts):
        body = lax.axis_index("body")
        bodies, near = near_bodies.shape
        cap = cycle_nodes.shape[2]
        modes, inc, nodes = incident.shape[1], incident.shape[3], incident.shape[4]
        slots = near * cap
        listed = near_bodies == body
        send_nodes = jnp.sum(jnp.where(listed[:, :, None], cycle_nodes, 0), axis=1)
        send_counts = jnp.sum(jnp.where(listed, cycle_counts, 0), axis=1)
        live = jnp.arange(cap, dtype=jnp.int32)[None, :] < send_counts[:, None]
        send_nodes = jnp.where(live, send_nodes, -1)
        order = target(body, jnp.asarray(dy), jnp.asarray(dz), bodies // ZDIM)
        node_row = send_nodes[order].reshape(1, bodies * cap)
        rows = modes * 2 * inc
        width = 256
        vmem = pl.BlockSpec(memory_space=pltpu.VMEM)
        hbm = pl.BlockSpec(memory_space=pl.ANY)
        out = pl.pallas_call(
            lambda *refs: kernel(n_mode, n_body, *refs),
            out_shape=jax.ShapeDtypeStruct((rows, nodes), BF),
            in_specs=[pl.BlockSpec(memory_space=pltpu.SMEM), vmem, vmem, vmem, vmem, vmem, hbm, hbm],
            out_specs=vmem,
            scratch_shapes=[
                pltpu.VMEM((modes, 2, nodes, nodes), BF),
                pltpu.VMEM((2, nodes, slots), BF),
                pltpu.VMEM((bodies * cap // width, nodes, width), BF),
                pltpu.VMEM((rows, nodes), BF),
                pltpu.VMEM((ITERS, bodies, rows // 2, 2 * cap), BF),
                pltpu.VMEM((bodies, rows // 2, 2 * cap), BF),
                pltpu.VMEM((bodies, rows // 2, 2 * cap), BF),
                pltpu.VMEM((slots // 128, rows, 128), F32),
                pltpu.VMEM((ITERS, n_mode, 2 * modes, slots), BF),
                pltpu.VMEM((ITERS, n_mode, 2 * modes, slots), BF),
                pltpu.VMEM((ITERS, n_mode, 2 * modes, nodes), BF),
                pltpu.VMEM((ITERS, n_mode, 2 * modes, nodes), BF),
                pltpu.VMEM((nodes // 128, rows, 128), F32),
                pltpu.VMEM((n_mode, NA // n_mode, slots), BF),
                pltpu.SemaphoreType.DMA((modes + 1,)),
                pltpu.SemaphoreType.DMA((3 * ITERS + 1,)),
                pltpu.SemaphoreType.DMA((3 * ITERS + 1,)),
            ],
            compiler_params=pltpu.CompilerParams(collective_id=0, has_side_effects=True),
            name="sweeps",
        )(
            near_bodies, node_row, jnp.asarray(up), jnp.asarray(down), incident[0], cycle_weight[0],
            inverse[0], coupling[0],
        )
        return out.reshape(1, modes, 2, inc, nodes)

    in_specs = (
        P("body", "mode", None, None, None),
        P("body", "mode", None, None, None),
        P("body", None, None, None),
        P("body", "mode", None),
        P(),
        P(),
        P(),
    )
    out_specs = P("body", "mode", None, None, None)
    return jax.shard_map(local, mesh=mesh, in_specs=in_specs, out_specs=out_specs, check_vma=False)
```

time: 454 us -> 57.1 us (0.13); the launches traced: 447 us -> 56.9 us
  local copies, waits for them, and re-layouts: 141 us -> 4.09 us
  waiting for transfers between devices: 109 us -> 0 us
  blocking collectives: 89.2 us -> 0 us
  other arithmetic: 68.9 us -> 2.47 us
  Pallas kernels: 0 us -> 50.3 us
  matrix products: 14.1 us -> 0 us
  between operations: 14 us -> 0.02 us
  starting transfers between devices: 9.94 us -> 0 us
    convert_element_type x9 -> x0, local copies, waits for them, and re-layouts: 77.7 us -> none  [the longest x2 49.2 us: local(): cycle_values.astype(jnp.float32) * weights[:, :, None, None]]
    reduce_scatter x2 -> x0, waiting for transfers between devices: 60.9 us -> none  [local(): lax.psum_scatter(jnp.einsum('qadi,adkc->kciq', near_field, downward_wide,...]
    all_to_all x1 -> x0, blocking collectives: 57.3 us -> none  [local(): lax.all_to_all(outgoing.reshape(bodies_all, -1), 'body', split_axis=0, co...]
    pallas_call x0 -> x1, Pallas kernels: none -> 50.3 us  [local(): pl.pallas_call(lambda *refs: kernel(n_mode, n_body, *refs), out_shape=jax...]
    all_to_all x1 -> x0, waiting for transfers between devices: 48.4 us -> none  [local(): lax.all_to_all(outgoing.reshape(bodies_all, -1), 'body', split_axis=0, co...]
    convert_element_type x5 -> x0, other arithmetic: 36.2 us -> none  [the longest x2 35.9 us: local(): (cycle_values.astype(jnp.float32) * weights[:, :, None, None]).astype(jnp...]
    all_gather x2 -> x0, blocking collectives: 31.9 us -> none  [local(): all_density = lax.all_gather(density, 'mode', axis=0, tiled=True)]
    select_n x6 -> x2, other arithmetic: 29.8 us -> 0.76 us  [the longest x1 0.68 us: local(): node_row = send_nodes[order].reshape(1, bodies * cap)]
  transfers between devices with their start and end apart: 3 -> 0, of which waited for: 3 -> 0; matrix products, arithmetic and copies ran while one was open for 0% -> 0% of each run, Pallas kernels for 0% -> 0%
where the time goes in v1:
time: 57.1 us; the launch traced here: 56.9 us
  Pallas kernels  50.3 us (88%)
  local copies, waits for them, and re-layouts  4.09 us (7%)
  other arithmetic  2.47 us (4%)
    pallas_call x1, Pallas kernels, local(): pl.pallas_call(lambda *refs: kernel(n_mode, n_body, *refs), out_shape=jax...  50.3 us
    unnamed x2, local copies, waits for them, and re-layouts  2.84 us

profile of v1, /device:TPU:1, one launch (start us, length us, event | category | flops | bytes accessed | tf_op | source)
XLA Modules:
  0.0 56.9 jit_solution(15725636352055702564)
XLA Ops:
  0.0 0.7 %compare_select_fusion = s32[32]{0:T(128)S(1)} fusion(s32[32]{0:T(128)} %constant.41.clone, s32[32]{0:T(128)} %constant.40.clone, s32[]{:T(128)S(6)} %rem.51, s32[]{:T(128)S(6)} %select_n.23), kind=kLoop, calls=%fused_computation.6 | loop fusion | flops 608 | bytes 392 | tf_op jit(solution)/shard_map/select_n | solution.py:226
  0.7 0.7 %select_reduce_fusion.1 = (s32[32]{0:T(128)S(1)}, pred[32,6]{0,1:T(8,128)(4,1)S(1)}) fusion(s32[32,6]{0,1:T(8,128)} %param.17, s32[32,6]{0,1:T(8,128)} %param.15, s32[]{:T(128)S(6)} %axis_index.12), kind=kLoop, calls=%fused_computation.5 | loop fusion | flops 544 | bytes 1860 | tf_op jit(solution)/shard_map/reduce_sum | solution.py:222
  1.4 1.0 %select_reduce_fusion = s32[32,64]{1,0:T(8,128)S(1)} fusion(s32[32,6,64]{2,0,1:T(8,128)} %param.16, pred[32,6]{0,1:T(8,128)(4,1)S(1)} %get-tuple-element.6), kind=kLoop, calls=%fused_computation.1 | loop fusion | flops 22528 | bytes 57536 | tf_op jit(solution)/shard_map/reduce_sum | solution.py:221
  2.4 0.1 fusion
  2.5 0.6 %gather_fusion = s32[32,64]{1,0:T(8,128)S(1)} fusion(s32[32,64]{1,0:T(8,128)S(1)} %fusion, s32[1024]{0:T(1024)S(1)} %pad_clamp_fusion), kind=kCustom, calls=%fused_computation | custom fusion | bytes 16512 | tf_op jit(solution)/shard_map/gather | solution.py:226
  3.1 0.7 %reshape.8.refs_1_ = s32[1,2048]{1,0:T(1,128)} reshape(s32[32,64]{1,0:T(8,128)S(1)} %gather_fusion) | data formatting | bytes 16384 | tf_op jit(solution)/shard_map/reshape | solution.py:226
  3.7 1.4 %copy.12.refs_0_ = s32[32,6]{1,0:T(8,128)} copy(s32[32,6]{0,1:T(8,128)} %param.15) | data formatting | bytes 1536 | tf_op args[4]
  5.1 50.3 %sweeps.1 = bf16[64,512]{1,0:T(8,128)(2,1)} custom-call(s32[32,6]{1,0:T(8,128)} %copy.12.refs_0_, s32[1,2048]{1,0:T(1,128)} %reshape.8.refs_1_, bf16[512,64]{1,0:T(8,128)(2,1)} %constant.42.clone.refs_2_, bf16[128,512]{1,0:T(8,128)(2,1)} %constant.43.clone.refs_3_, bf16[4,2,8,512]{3,2,1,0:T(8,128)(2,1)} %bitcast.8, bf16[32,384]{1,0:T(8,128)(2,1)} %bitcast.9, ...), custom_call_target="tpu_custom_call" | custom-call | tf_op jit(solution)/shard_map/sweeps/pallas_call | solution.py:231
  55.4 1.5 %copy.14 = bf16[1,4,2,8,512]{4,3,2,1,0:T(8,128)(2,1)} copy(bf16[1,4,2,8,512]{4,3,2,1,0:T(8,128)(2,1)} %bitcast.7) | data formatting | bytes 131072
  (1 shorter events, 0.0 us)

commit v2 on v1

v2 whole, which is shorter than its diff:
```python
import math

import jax
import jax.numpy as jnp
import numpy as np
from jax import lax
from jax.experimental import pallas as pl
from jax.experimental.pallas import tpu as pltpu
from jax.sharding import PartitionSpec as P

MODES = 32
NA = 256
ITERS = 2
ZDIM = 8
MESH = pl.DeviceIdType.MESH
BF = jnp.bfloat16
F32 = jnp.float32


def tables():
    wavenum = np.arange(MODES) - MODES // 2
    residue = (wavenum[:, None] * np.arange(NA)[None, :]) % NA
    theta = residue.astype(np.float32) * np.float32(2.0 * math.pi / NA)
    cos, sin = np.cos(theta), np.sin(theta)
    up = np.stack([np.stack([cos, sin], -1), np.stack([-sin, cos], -1)], 1)
    up = up.transpose(3, 2, 0, 1).reshape(2 * NA, 2 * MODES)
    down = np.stack([np.stack([cos, sin], 1), np.stack([-sin, cos], 1)], 1)
    turned = np.stack([-down[:, 1], down[:, 0]], 1)
    down = np.concatenate([down.reshape(2 * MODES, 2 * NA), turned.reshape(2 * MODES, 2 * NA)], 0)
    return up.astype(BF), down.astype(BF)


def offsets(bodies):
    ydim = bodies // ZDIM
    far = lambda d, n: min(d, n - d)
    order = [(dy, dz) for dy in range(ydim) for dz in range(ZDIM)]
    order.sort(key=lambda o: (-far(o[0], ydim), -far(o[1], ZDIM), o))
    return order


def target(body, dy, dz, ydim):
    return lax.rem(body // ZDIM + dy, ydim) * ZDIM + lax.rem(lax.rem(body, ZDIM) + dz, ZDIM)


def dot_nt(left, right):
    return lax.dot_general(left, right, (((1,), (1,)), ((), ())), preferred_element_type=F32)


def kernel(
    n_mode, n_body, near_hbm, counts_hbm, nodes_hbm, up_hbm, down_hbm, inc_hbm, w_hbm, inv_hbm, coup_hbm,
    out_ref,
    near_s, near_v, counts_v, nodes_v, up_v, down_v, inc_v, w_v, inv_v, coup_v,
    picks, onehot, dbuf, dens, snd1, recv1a, recv1b, snd3, recv3, rbuf, wall,
    load_sem, send_sem, recv_sem, ready_sem,
):
    me = lax.axis_index("mode")
    body = lax.axis_index("body")
    ydim = n_body // ZDIM
    modes, incs = inv_v.shape[0], inc_v.shape[2]
    near, cap = nodes_v.shape[0], nodes_v.shape[2]
    tiles = rbuf.shape[0]
    order = offsets(n_body)

    pairs = [(inc_hbm, inc_v), (near_hbm, near_v), (counts_hbm, counts_v), (nodes_hbm, nodes_v)]
    pairs += [(inv_hbm.at[k], inv_v.at[k]) for k in range(modes)]
    pairs += [(near_hbm, near_s), (up_hbm, up_v), (down_hbm, down_v), (w_hbm, w_v), (coup_hbm, coup_v)]
    loads = [pltpu.make_async_copy(src, dst, load_sem.at[j]) for j, (src, dst) in enumerate(pairs)]
    load_inc, load_near, load_counts, load_nodes = loads[:4]
    load_inv, (load_near_s, load_up, load_down, load_w, load_coup) = loads[4 : 4 + modes], loads[4 + modes :]

    barrier = pltpu.get_barrier_semaphore()
    for dy, dz in order[:-1]:
        pl.semaphore_signal(
            barrier, inc=1, device_id={"body": target(body, dy, dz, ydim)}, device_id_type=MESH
        )
    for off in range(1, n_mode):
        pl.semaphore_signal(
            barrier, inc=1, device_id={"mode": lax.rem(me + off, n_mode)}, device_id_type=MESH
        )
    for load in loads:
        load.start()

    load_near.wait()
    load_counts.wait()
    load_nodes.wait()
    near_t = jnp.transpose(near_v[...])
    counts_t = jnp.transpose(counts_v[...])
    slot = lax.broadcasted_iota(jnp.int32, (n_body, cap), 1)
    chosen = jnp.full((n_body, cap), -1, jnp.int32)
    for n in range(near):
        ours = jnp.broadcast_to(near_t[:, n : n + 1], (n_body, cap)) == body
        live = slot < jnp.broadcast_to(counts_t[:, n : n + 1], (n_body, cap))
        chosen = jnp.where(ours & live, nodes_v[n], chosen)
    picks[...] = jnp.concatenate([chosen, chosen], 1)

    groups, width = onehot.shape[0], onehot.shape[2]
    per_group = width // cap
    node_index = lax.broadcasted_iota(jnp.int32, (onehot.shape[1], 2 * cap), 0)
    low = lax.broadcasted_iota(jnp.int32, (1, 2 * cap), 1) < cap
    for r in range(0, n_body, 2):
        first, second = (picks[pl.ds(target(body, *order[r + j], ydim), 1), :] for j in range(2))
        row = jnp.where(low, first, second)
        lanes = (r % per_group) * cap
        onehot[r // per_group, :, lanes : lanes + 2 * cap] = jnp.where(node_index == row, 1.0, 0.0).astype(BF)

    def arrived(dst, slot):
        pltpu.make_async_copy(dst, dst, recv_sem.at[slot]).wait()

    def sent(part, slot):
        pltpu.make_async_copy(part, part, send_sem.at[slot]).wait()

    shape = (n_mode, 2 * modes, 2 * cap)
    keep = (lax.broadcasted_iota(jnp.int32, shape, 1) < modes) == (lax.broadcasted_iota(jnp.int32, shape, 2) < cap)

    def swap_quadrants(block):
        return jnp.where(keep, block, pltpu.roll(pltpu.roll(block, modes, 1), cap, 2))

    def inverse_product(k, real, imag):
        first = jnp.concatenate([real, imag], 0).astype(BF)
        second = jnp.concatenate([-imag, real], 0).astype(BF)
        return dot_nt(first, inv_v[k, 0]) + dot_nt(second, inv_v[k, 1])

    def hold(k, value):
        for q in range(tiles):
            dbuf[q, 2 * incs * k : 2 * incs * (k + 1)] = value[:, 128 * q : 128 * q + 128]

    load_inc.wait()
    for k in range(modes):
        load_inv[k].wait()
        hold(k, inverse_product(k, inc_v[k, 0].astype(F32), inc_v[k, 1].astype(F32)))

    for it in range(ITERS):
        to_body, from_body = snd1.at[it], (recv1a, recv1b)[it]

        def send_group(g, it=it, to_body=to_body, from_body=from_body):
            for r in range(g * per_group, (g + 1) * per_group):
                there = target(body, *order[r], ydim)
                last = r == n_body - 1
                for off in range(1 if last else 0, n_mode):
                    peer = lax.rem(me + off, n_mode)
                    pltpu.make_async_remote_copy(
                        src_ref=to_body.at[r, peer], dst_ref=from_body.at[body, me],
                        send_sem=send_sem.at[2 * it], recv_sem=recv_sem.at[2 * it],
                        device_id={"mode": peer, "body": there}, device_id_type=MESH,
                    ).start()
                if last:
                    pltpu.make_async_copy(
                        to_body.at[r, me], from_body.at[body, me], recv_sem.at[2 * it]
                    ).start()

        for i in range(incs):
            rows = [dbuf[q, pl.ds(i, 2 * modes, stride=incs), :] for q in range(tiles)]
            dens[2 * modes * i : 2 * modes * (i + 1)] = jnp.concatenate(rows, 1)
        all_dens = dens[...].astype(BF)

        if it == 0:
            pl.semaphore_wait(barrier, n_body + n_mode - 2)
            for off in range(1, n_mode):
                pl.semaphore_signal(
                    ready_sem, inc=1, device_id={"mode": lax.rem(me + off, n_mode)}, device_id_type=MESH
                )
        for g in range(groups):
            picked = jnp.dot(all_dens, onehot[g], preferred_element_type=F32)
            for pair in range(per_group // 2):
                part = picked[:, 128 * pair : 128 * pair + 128].reshape(shape)
                part = swap_quadrants(part).astype(BF)
                r = g * per_group + 2 * pair
                snd1[it, r] = part[:, :modes]
                snd1[it, r + 1] = part[:, modes:]
            if it == 0 and g == 1:
                pl.semaphore_wait(ready_sem, n_mode - 1)
            if g > 0:
                send_group(g - 1)
        send_group(groups - 1)

        if it == 0:
            load_w.wait()
            for off in range(1, n_mode):
                pltpu.make_async_remote_copy(
                    src_ref=w_v, dst_ref=wall.at[me], send_sem=send_sem.at[4], recv_sem=recv_sem.at[4],
                    device_id={"mode": lax.rem(me + off, n_mode)}, device_id_type=MESH,
                ).start()
            pltpu.make_async_copy(w_v, wall.at[me], recv_sem.at[4]).start()
            load_near_s.wait()
            load_up.wait()
            load_down.wait()
            load_coup.wait()

        arrived(from_body, 2 * it)
        modal = []
        for v in range(0, near, 2):
            both = [from_body[near_s[v + j, body]].astype(F32) for j in range(2)]
            modal.append(swap_quadrants(jnp.concatenate(both, 1)).reshape(2 * MODES, 2 * cap))
        modal = jnp.concatenate(modal, 1).astype(BF)
        cycles = jnp.dot(up_v[...], modal, preferred_element_type=F32)
        if it == 0:
            arrived(wall, 4)
        weights = wall[...].astype(F32).reshape(NA, -1)
        scaled = jnp.concatenate([cycles[:NA] * weights, cycles[NA:] * weights], 0).astype(BF)
        back = jnp.dot(down_v[...], scaled, preferred_element_type=F32).astype(BF)
        half = back.shape[0] // 2
        correction = dot_nt(back[:half], coup_v[0]) + dot_nt(back[half:], coup_v[1])
        for j in range(n_mode):
            snd3[it, j] = correction[2 * modes * j : 2 * modes * (j + 1)].astype(BF)
        for off in range(1, n_mode):
            peer = lax.rem(me + off, n_mode)
            pltpu.make_async_remote_copy(
                src_ref=snd3.at[it, peer], dst_ref=recv3.at[it, me], send_sem=send_sem.at[2 * it + 1],
                recv_sem=recv_sem.at[2 * it + 1], device_id={"mode": peer}, device_id_type=MESH,
            ).start()
        pltpu.make_async_copy(snd3.at[it, me], recv3.at[it, me], recv_sem.at[2 * it + 1]).start()
        arrived(recv3.at[it], 2 * it + 1)

        for i in range(incs):
            value = recv3[it, i].astype(F32)
            for q in range(tiles):
                rbuf[q, 2 * modes * i : 2 * modes * (i + 1)] = value[:, 128 * q : 128 * q + 128]
        for k in range(modes):
            sides = []
            for c in range(2):
                value = [rbuf[q, pl.ds(2 * k + c, incs, stride=2 * modes), :] for q in range(tiles)]
                value = jnp.concatenate(value, 1)
                sides.append(inc_v[k, c].astype(F32) - value * (1.0 / NA))
            value = inverse_product(k, *sides)
            if it < ITERS - 1:
                hold(k, value)
            else:
                out_ref[2 * incs * k : 2 * incs * (k + 1)] = value.astype(BF)

    for it in range(ITERS):
        sent(snd1.at[it, pl.ds(0, n_body - 1)], 2 * it)
        sent(snd1.at[it, n_body - 1, pl.ds(0, n_mode - 1)], 2 * it)
        sent(snd3.at[it, pl.ds(0, n_mode - 1)], 2 * it + 1)
    sent(wall.at[pl.ds(0, n_mode - 1)], 4)


def solution(mesh):
    n_mode, n_body = mesh.shape["mode"], mesh.shape["body"]
    up, down = tables()

    def local(incident, inverse, coupling, cycle_weight, near_bodies, cycle_nodes, cycle_counts):
        bodies, near = near_bodies.shape
        cap = cycle_nodes.shape[2]
        modes, inc, nodes = incident.shape[1], incident.shape[3], incident.shape[4]
        slots = near * cap
        rows = modes * 2 * inc
        width = 4 * cap
        hbm = pl.BlockSpec(memory_space=pl.ANY)
        out = pl.pallas_call(
            lambda *refs: kernel(n_mode, n_body, *refs),
            out_shape=jax.ShapeDtypeStruct((rows, nodes), BF),
            in_specs=[hbm] * 9,
            out_specs=pl.BlockSpec(memory_space=pltpu.VMEM),
            scratch_shapes=[
                pltpu.SMEM((near, bodies), jnp.int32),
                pltpu.VMEM((near, bodies), jnp.int32),
                pltpu.VMEM((near, bodies), jnp.int32),
                pltpu.VMEM((near, bodies, cap), jnp.int32),
                pltpu.VMEM((2 * NA, 2 * MODES), BF),
                pltpu.VMEM((4 * MODES, 2 * NA), BF),
                pltpu.VMEM((modes, 2, inc, nodes), BF),
                pltpu.VMEM((NA // n_mode, slots), BF),
                pltpu.VMEM((modes, 2, nodes, nodes), BF),
                pltpu.VMEM((2, nodes, slots), BF),
                pltpu.VMEM((bodies, 2 * cap), jnp.int32),
                pltpu.VMEM((bodies * cap // width, nodes, width), BF),
                pltpu.VMEM((nodes // 128, rows, 128), F32),
                pltpu.VMEM((rows, nodes), F32),
                pltpu.VMEM((ITERS, bodies, n_mode, modes, 2 * cap), BF),
                pltpu.VMEM((bodies, n_mode, modes, 2 * cap), BF),
                pltpu.VMEM((bodies, n_mode, modes, 2 * cap), BF),
                pltpu.VMEM((ITERS, n_mode, 2 * modes, nodes), BF),
                pltpu.VMEM((ITERS, n_mode, 2 * modes, nodes), BF),
                pltpu.VMEM((nodes // 128, rows, 128), F32),
                pltpu.VMEM((n_mode, NA // n_mode, slots), BF),
                pltpu.SemaphoreType.DMA((modes + 9,)),
                pltpu.SemaphoreType.DMA((2 * ITERS + 1,)),
                pltpu.SemaphoreType.DMA((2 * ITERS + 1,)),
                pltpu.SemaphoreType.REGULAR,
            ],
            compiler_params=pltpu.CompilerParams(collective_id=0, has_side_effects=True),
            name="sweeps",
        )(
            near_bodies.T, cycle_counts.T, cycle_nodes.transpose(1, 0, 2), jnp.asarray(up), jnp.asarray(down),
            incident[0], cycle_weight[0], inverse[0], coupling[0],
        )
        return out.reshape(1, modes, 2, inc, nodes)

    in_specs = (
        P("body", "mode", None, None, None),
        P("body", "mode", None, None, None),
        P("body", None, None, None),
        P("body", "mode", None),
        P(),
        P(),
        P(),
    )
    out_specs = P("body", "mode", None, None, None)
    return jax.shard_map(local, mesh=mesh, in_specs=in_specs, out_specs=out_specs, check_vma=False)
```

time: 57.1 us -> 48.1 us (0.84)
  Pallas kernels: 50.3 us -> 46.5 us
  local copies, waits for them, and re-layouts: 4.09 us -> 1.47 us
  other arithmetic: 2.47 us -> 0 us
    pallas_call x1, Pallas kernels: 50.3 us -> 46.5 us  [local(): pl.pallas_call(lambda *refs: kernel(n_mode, n_body, *refs), out_shape=jax...]
    reduce_sum x2 -> x0, other arithmetic: 1.71 us -> none  [the longest x1 0.99 us: local(): send_nodes = jnp.sum(jnp.where(listed[:, :, None], cycle_nodes, 0), axis=1)]
    unnamed x2 -> x1, local copies, waits for them, and re-layouts: 2.84 us -> 1.47 us
    select_n x2 -> x0, other arithmetic: 0.76 us -> none  [the longest x1 0.68 us: local(): node_row = send_nodes[order].reshape(1, bodies * cap)]
    reshape x1 -> x0, local copies, waits for them, and re-layouts: 0.67 us -> none  [local(): node_row = send_nodes[order].reshape(1, bodies * cap)]
    gather x1 -> x0, local copies, waits for them, and re-layouts: 0.57 us -> none  [local(): node_row = send_nodes[order].reshape(1, bodies * cap)]
where the time goes in v2:
time: 48.1 us; the launch traced here: 48 us
  Pallas kernels  46.5 us (97%)
  local copies, waits for them, and re-layouts  1.47 us (3%)
    pallas_call x1, Pallas kernels, local(): pl.pallas_call(lambda *refs: kernel(n_mode, n_body, *refs), out_shape=jax...  46.5 us
    unnamed x1, local copies, waits for them, and re-layouts  1.47 us

profile of v2, /device:TPU:1, one launch (start us, length us, event | category | flops | bytes accessed | tf_op | source)
XLA Modules:
  0.0 48.0 jit_solution(16722034676813547436)
XLA Ops:
  0.0 46.5 %sweeps.1 = bf16[64,512]{1,0:T(8,128)(2,1)} custom-call(s32[6,32]{1,0:T(8,128)} %bitcast.14, s32[6,32]{1,0:T(8,128)} %bitcast.15, s32[6,32,64]{2,1,0:T(8,128)} %bitcast.11, bf16[512,64]{1,0:T(8,128)(2,1)} %constant.4.clone.refs_3_, bf16[128,512]{1,0:T(8,128)(2,1)} %constant.5.clone.refs_4_, bf16[4,2,8,512]{3,2,1,0:T(8,128)(2,1)} %bitcast.12, ...), custom_call_target="tpu_custom_call" | custom-call | tf_op jit(solution)/shard_map/sweeps/pallas_call | solution.py:249
  46.5 1.5 %copy.11 = bf16[1,4,2,8,512]{4,3,2,1,0:T(8,128)(2,1)} copy(bf16[1,4,2,8,512]{4,3,2,1,0:T(8,128)(2,1)} %bitcast.10) | data formatting | bytes 131072

commit v3 on v2

--- a/solution.py
+++ b/solution.py
@@ -55,11 +55,17 @@
 ):
     me = lax.axis_index("mode")
     body = lax.axis_index("body")
+    xdim = n_mode // 2
+    x, core = me // 2, lax.rem(me, 2)
+    mine = core * xdim + x
     ydim = n_body // ZDIM
     modes, incs = inv_v.shape[0], inc_v.shape[2]
+    part = incs // 2
     near, cap = nodes_v.shape[0], nodes_v.shape[2]
-    tiles = rbuf.shape[0]
+    tiles = rbuf.shape[1]
     order = offsets(n_body)
+    across = sorted(range(xdim), key=lambda dx: -min(dx, xdim - dx))
+    peers = sorted(range(1, n_mode), key=lambda off: -min(off, n_mode - off))
 
     pairs = [(inc_hbm, inc_v), (near_hbm, near_v), (counts_hbm, counts_v), (nodes_hbm, nodes_v)]
     pairs += [(inv_hbm.at[k], inv_v.at[k]) for k in range(modes)]
@@ -73,7 +79,7 @@
         pl.semaphore_signal(
             barrier, inc=1, device_id={"body": target(body, dy, dz, ydim)}, device_id_type=MESH
         )
-    for off in range(1, n_mode):
+    for off in peers:
         pl.semaphore_signal(
             barrier, inc=1, device_id={"mode": lax.rem(me + off, n_mode)}, device_id_type=MESH
         )
@@ -106,87 +112,96 @@
     def arrived(dst, slot):
         pltpu.make_async_copy(dst, dst, recv_sem.at[slot]).wait()
 
-    def sent(part, slot):
-        pltpu.make_async_copy(part, part, send_sem.at[slot]).wait()
-
-    shape = (n_mode, 2 * modes, 2 * cap)
-    keep = (lax.broadcasted_iota(jnp.int32, shape, 1) < modes) == (lax.broadcasted_iota(jnp.int32, shape, 2) < cap)
+    def sent(block, slot):
+        pltpu.make_async_copy(block, block, send_sem.at[slot]).wait()
 
     def swap_quadrants(block):
-        return jnp.where(keep, block, pltpu.roll(pltpu.roll(block, modes, 1), cap, 2))
-
-    def inverse_product(k, real, imag):
-        first = jnp.concatenate([real, imag], 0).astype(BF)
-        second = jnp.concatenate([-imag, real], 0).astype(BF)
+        up_half = lax.broadcasted_iota(jnp.int32, block.shape, 1) < modes
+        left_half = lax.broadcasted_iota(jnp.int32, block.shape, 2) < cap
+        return jnp.where(up_half == left_half, block, pltpu.roll(pltpu.roll(block, modes, 1), cap, 2))
+
+    def inverse_product(k, sides):
+        first = jnp.concatenate([v for real, imag in sides for v in (real, imag)], 0).astype(BF)
+        second = jnp.concatenate([v for real, imag in sides for v in (-imag, real)], 0).astype(BF)
         return dot_nt(first, inv_v[k, 0]) + dot_nt(second, inv_v[k, 1])
 
-    def hold(k, value):
+    def hold(k, h, value):
         for q in range(tiles):
-            dbuf[q, 2 * incs * k : 2 * incs * (k + 1)] = value[:, 128 * q : 128 * q + 128]
+            dbuf[h, q, 2 * part * k : 2 * part * (k + 1)] = value[:, 128 * q : 128 * q + 128]
+
+    def density_rows(h):
+        for i in range(part):
+            rows = [dbuf[h, q, pl.ds(i, 2 * modes, stride=part), :] for q in range(tiles)]
+            dens[h, 2 * modes * i : 2 * modes * (i + 1)] = jnp.concatenate(rows, 1)
+        return dens[h].astype(BF)
+
+    def gather(it, h, g, rows):
+        picked = jnp.dot(rows, onehot[g], preferred_element_type=F32)
+        for pair in range(per_group // 2):
+            block = picked[:, 128 * pair : 128 * pair + 128].reshape(part, 2 * modes, 2 * cap)
+            block = swap_quadrants(block).astype(BF)
+            r = g * per_group + 2 * pair
+            snd1[it, r, part * h : part * (h + 1)] = block[:, :modes]
+            snd1[it, r + 1, part * h : part * (h + 1)] = block[:, modes:]
+
+    def post(it, r, to_x, to_core):
+        pltpu.make_async_remote_copy(
+            src_ref=snd1.at[it, r, to_core * xdim + to_x], dst_ref=(recv1a, recv1b)[it].at[body, me],
+            send_sem=send_sem.at[2 * it], recv_sem=recv_sem.at[it],
+            device_id={"mode": 2 * to_x + to_core, "body": target(body, *order[r], ydim)},
+            device_id_type=MESH,
+        ).start()
+
+    def keep_own(it):
+        pltpu.make_async_copy(
+            snd1.at[it, n_body - 1, mine], (recv1a, recv1b)[it].at[body, me], recv_sem.at[it]
+        ).start()
 
     load_inc.wait()
     for k in range(modes):
         load_inv[k].wait()
-        hold(k, inverse_product(k, inc_v[k, 0].astype(F32), inc_v[k, 1].astype(F32)))
+        real, imag = inc_v[k, 0].astype(F32), inc_v[k, 1].astype(F32)
+        cut = [slice(part * h, part * (h + 1)) for h in range(2)]
+        value = inverse_product(k, [(real[c], imag[c]) for c in cut])
+        for h in range(2):
+            hold(k, h, value[2 * part * h : 2 * part * (h + 1)])
+    for h in range(2):
+        rows = density_rows(h)
+        for g in range(groups):
+            gather(0, h, g, rows)
+
+    pl.semaphore_wait(barrier, n_body + n_mode - 2)
+    for off in peers:
+        pl.semaphore_signal(
+            ready_sem, inc=1, device_id={"mode": lax.rem(me + off, n_mode)}, device_id_type=MESH
+        )
+    for r in range(n_body - 1):
+        post(0, r, x, core)
+    pl.semaphore_wait(ready_sem, n_mode - 1)
+    for h in range(2):
+        for r in range(n_body):
+            for dx in across[:-1]:
+                post(0, r, lax.rem(x + dx, xdim), h)
+        if h == 0:
+            for r in range(n_body):
+                post(0, r, x, 1 - core)
+    keep_own(0)
+
+    load_w.wait()
+    for off in peers:
+        pltpu.make_async_remote_copy(
+            src_ref=w_v, dst_ref=wall.at[me], send_sem=send_sem.at[4], recv_sem=recv_sem.at[6],
+            device_id={"mode": lax.rem(me + off, n_mode)}, device_id_type=MESH,
+        ).start()
+    pltpu.make_async_copy(w_v, wall.at[me], recv_sem.at[6]).start()
+    load_near_s.wait()
+    load_up.wait()
+    load_down.wait()
+    load_coup.wait()
 
     for it in range(ITERS):
-        to_body, from_body = snd1.at[it], (recv1a, recv1b)[it]
-
-        def send_group(g, it=it, to_body=to_body, from_body=from_body):
-            for r in range(g * per_group, (g + 1) * per_group):
-                there = target(body, *order[r], ydim)
-                last = r == n_body - 1
-                for off in range(1 if last else 0, n_mode):
-                    peer = lax.rem(me + off, n_mode)
-                    pltpu.make_async_remote_copy(
-                        src_ref=to_body.at[r, peer], dst_ref=from_body.at[body, me],
-                        send_sem=send_sem.at[2 * it], recv_sem=recv_sem.at[2 * it],
-                        device_id={"mode": peer, "body": there}, device_id_type=MESH,
-                    ).start()
-                if last:
-                    pltpu.make_async_copy(
-                        to_body.at[r, me], from_body.at[body, me], recv_sem.at[2 * it]
-                    ).start()
-
-        for i in range(incs):
-            rows = [dbuf[q, pl.ds(i, 2 * modes, stride=incs), :] for q in range(tiles)]
-            dens[2 * modes * i : 2 * modes * (i + 1)] = jnp.concatenate(rows, 1)
-        all_dens = dens[...].astype(BF)
-
-        if it == 0:
-            pl.semaphore_wait(barrier, n_body + n_mode - 2)
-            for off in range(1, n_mode):
-                pl.semaphore_signal(
-                    ready_sem, inc=1, device_id={"mode": lax.rem(me + off, n_mode)}, device_id_type=MESH
-                )
-        for g in range(groups):
-            picked = jnp.dot(all_dens, onehot[g], preferred_element_type=F32)
-            for pair in range(per_group // 2):
-                part = picked[:, 128 * pair : 128 * pair + 128].reshape(shape)
-                part = swap_quadrants(part).astype(BF)
-                r = g * per_group + 2 * pair
-                snd1[it, r] = part[:, :modes]
-                snd1[it, r + 1] = part[:, modes:]
-            if it == 0 and g == 1:
-                pl.semaphore_wait(ready_sem, n_mode - 1)
-            if g > 0:
-                send_group(g - 1)
-        send_group(groups - 1)
-
-        if it == 0:
-            load_w.wait()
-            for off in range(1, n_mode):
-                pltpu.make_async_remote_copy(
-                    src_ref=w_v, dst_ref=wall.at[me], send_sem=send_sem.at[4], recv_sem=recv_sem.at[4],
-                    device_id={"mode": lax.rem(me + off, n_mode)}, device_id_type=MESH,
-                ).start()
-            pltpu.make_async_copy(w_v, wall.at[me], recv_sem.at[4]).start()
-            load_near_s.wait()
-            load_up.wait()
-            load_down.wait()
-            load_coup.wait()
-
-        arrived(from_body, 2 * it)
+        from_body = (recv1a, recv1b)[it]
+        arrived(from_body, it)
         modal = []
         for v in range(0, near, 2):
             both = [from_body[near_s[v + j, body]].astype(F32) for j in range(2)]
@@ -194,7 +209,7 @@
         modal = jnp.concatenate(modal, 1).astype(BF)
         cycles = jnp.dot(up_v[...], modal, preferred_element_type=F32)
         if it == 0:
-            arrived(wall, 4)
+            arrived(wall, 6)
         weights = wall[...].astype(F32).reshape(NA, -1)
         scaled = jnp.concatenate([cycles[:NA] * weights, cycles[NA:] * weights], 0).astype(BF)
         back = jnp.dot(down_v[...], scaled, preferred_element_type=F32).astype(BF)
@@ -202,30 +217,48 @@
         correction = dot_nt(back[:half], coup_v[0]) + dot_nt(back[half:], coup_v[1])
         for j in range(n_mode):
             snd3[it, j] = correction[2 * modes * j : 2 * modes * (j + 1)].astype(BF)
-        for off in range(1, n_mode):
+        for off in peers:
             peer = lax.rem(me + off, n_mode)
             pltpu.make_async_remote_copy(
-                src_ref=snd3.at[it, peer], dst_ref=recv3.at[it, me], send_sem=send_sem.at[2 * it + 1],
-                recv_sem=recv_sem.at[2 * it + 1], device_id={"mode": peer}, device_id_type=MESH,
+                src_ref=snd3.at[it, peer], dst_ref=recv3.at[it, mine], send_sem=send_sem.at[2 * it + 1],
+                recv_sem=recv_sem.at[2 + 2 * it + core], device_id={"mode": peer}, device_id_type=MESH,
             ).start()
-        pltpu.make_async_copy(snd3.at[it, me], recv3.at[it, me], recv_sem.at[2 * it + 1]).start()
-        arrived(recv3.at[it], 2 * it + 1)
-
-        for i in range(incs):
-            value = recv3[it, i].astype(F32)
-            for q in range(tiles):
-                rbuf[q, 2 * modes * i : 2 * modes * (i + 1)] = value[:, 128 * q : 128 * q + 128]
-        for k in range(modes):
-            sides = []
-            for c in range(2):
-                value = [rbuf[q, pl.ds(2 * k + c, incs, stride=2 * modes), :] for q in range(tiles)]
-                value = jnp.concatenate(value, 1)
-                sides.append(inc_v[k, c].astype(F32) - value * (1.0 / NA))
-            value = inverse_product(k, *sides)
+        pltpu.make_async_copy(snd3.at[it, me], recv3.at[it, mine], recv_sem.at[2 + 2 * it + core]).start()
+
+        for h in range(2):
+            arrived(recv3.at[it, pl.ds(part * h, part)], 2 + 2 * it + h)
+            for i in range(part):
+                value = recv3[it, part * h + i].astype(F32)
+                for q in range(tiles):
+                    rbuf[h, q, 2 * modes * i : 2 * modes * (i + 1)] = value[:, 128 * q : 128 * q + 128]
+            for k in range(modes):
+                sides = []
+                for c in range(2):
+                    value = [rbuf[h, q, pl.ds(2 * k + c, part, stride=2 * modes), :] for q in range(tiles)]
+                    value = jnp.concatenate(value, 1)
+                    source = inc_v[k, c].astype(F32)[part * h : part * (h + 1)]
+                    sides.append(source - value * (1.0 / NA))
+                value = inverse_product(k, [sides])
+                if it == ITERS - 1 and h == 1:
+                    early = [dbuf[0, q, 2 * part * k : 2 * part * (k + 1)] for q in range(tiles)]
+                    early = jnp.concatenate(early, 1)
+                    value = [early[:part], value[:part], early[part:], value[part:]]
+                    value = jnp.concatenate(value, 0)
+                    out_ref[2 * incs * k : 2 * incs * (k + 1)] = value.astype(BF)
+                else:
+                    hold(k, h, value)
             if it < ITERS - 1:
-                hold(k, value)
-            else:
-                out_ref[2 * incs * k : 2 * incs * (k + 1)] = value.astype(BF)
+                rows = density_rows(h)
+                for g in range(groups + 1):
+                    if g < groups:
+                        gather(it + 1, h, g, rows)
+                    if g > 0:
+                        for r in range((g - 1) * per_group, g * per_group):
+                            for dx in across if r < n_body - 1 else across[:-1]:
+                                post(it + 1, r, lax.rem(x + dx, xdim), h)
+                if h == 1:
+                    post(it + 1, n_body - 1, x, 1 - core)
+                    keep_own(it + 1)
 
     for it in range(ITERS):
         sent(snd1.at[it, pl.ds(0, n_body - 1)], 2 * it)
@@ -248,7 +281,7 @@
         hbm = pl.BlockSpec(memory_space=pl.ANY)
         out = pl.pallas_call(
             lambda *refs: kernel(n_mode, n_body, *refs),
-            out_shape=jax.ShapeDtypeStruct((rows, nodes), BF),
+            out_shape=pltpu.VMEM((rows, nodes), BF),
             in_specs=[hbm] * 9,
             out_specs=pl.BlockSpec(memory_space=pltpu.VMEM),
             scratch_shapes=[
@@ -264,18 +297,18 @@
                 pltpu.VMEM((2, nodes, slots), BF),
                 pltpu.VMEM((bodies, 2 * cap), jnp.int32),
                 pltpu.VMEM((bodies * cap // width, nodes, width), BF),
-                pltpu.VMEM((nodes // 128, rows, 128), F32),
-                pltpu.VMEM((rows, nodes), F32),
+                pltpu.VMEM((2, nodes // 128, rows // 2, 128), F32),
+                pltpu.VMEM((2, rows // 2, nodes), F32),
                 pltpu.VMEM((ITERS, bodies, n_mode, modes, 2 * cap), BF),
                 pltpu.VMEM((bodies, n_mode, modes, 2 * cap), BF),
                 pltpu.VMEM((bodies, n_mode, modes, 2 * cap), BF),
                 pltpu.VMEM((ITERS, n_mode, 2 * modes, nodes), BF),
                 pltpu.VMEM((ITERS, n_mode, 2 * modes, nodes), BF),
-                pltpu.VMEM((nodes // 128, rows, 128), F32),
+                pltpu.VMEM((2, nodes // 128, rows // 2, 128), F32),
                 pltpu.VMEM((n_mode, NA // n_mode, slots), BF),
                 pltpu.SemaphoreType.DMA((modes + 9,)),
                 pltpu.SemaphoreType.DMA((2 * ITERS + 1,)),
-                pltpu.SemaphoreType.DMA((2 * ITERS + 1,)),
+                pltpu.SemaphoreType.DMA((3 * ITERS + 1,)),
                 pltpu.SemaphoreType.REGULAR,
             ],
             compiler_params=pltpu.CompilerParams(collective_id=0, has_side_effects=True),

time: 48.1 us -> 44.1 us (0.917)
  Pallas kernels: 46.5 us -> 43.4 us
  local copies, waits for them, and re-layouts: 1.47 us -> 0.63 us
    pallas_call x1, Pallas kernels: 46.5 us -> 43.4 us  [local(): pl.pallas_call(lambda *refs: kernel(n_mode, n_body, *refs), out_shape=plt...]
    unnamed x1, local copies, waits for them, and re-layouts: 1.47 us -> 0.63 us
where the time goes in v3:
time: 44.1 us
  Pallas kernels  43.4 us (98%)
  local copies, waits for them, and re-layouts  0.63 us (1%)
    pallas_call x1, Pallas kernels, local(): pl.pallas_call(lambda *refs: kernel(n_mode, n_body, *refs), out_shape=plt...  43.4 us

profile of v3, /device:TPU:1, one launch (start us, length us, event | category | flops | bytes accessed | tf_op | source)
XLA Modules:
  0.0 44.1 jit_solution(6754748853160623555)
XLA Ops:
  0.0 43.4 %sweeps.1 = bf16[64,512]{1,0:T(8,128)(2,1)S(1)} custom-call(s32[6,32]{1,0:T(8,128)} %bitcast.14, s32[6,32]{1,0:T(8,128)} %bitcast.15, s32[6,32,64]{2,1,0:T(8,128)} %bitcast.11, bf16[512,64]{1,0:T(8,128)(2,1)} %constant.4.clone.refs_3_, bf16[128,512]{1,0:T(8,128)(2,1)} %constant.5.clone.refs_4_, bf16[4,2,8,512]{3,2,1,0:T(8,128)(2,1)} %bitcast.12, ...), custom_call_target="tpu_custom_call" | custom-call | tf_op jit(solution)/shard_map/sweeps/pallas_call | solution.py:282
  43.4 0.6 %copy.11 = bf16[1,4,2,8,512]{4,3,2,1,0:T(8,128)(2,1)} copy(bf16[1,4,2,8,512]{4,3,2,1,0:T(8,128)(2,1)S(1)} %bitcast.8) | data formatting | bytes 131072

commit v4 on v3

--- a/solution.py
+++ b/solution.py
@@ -49,7 +49,7 @@
 def kernel(
     n_mode, n_body, near_hbm, counts_hbm, nodes_hbm, up_hbm, down_hbm, inc_hbm, w_hbm, inv_hbm, coup_hbm,
     out_ref,
-    near_s, near_v, counts_v, nodes_v, up_v, down_v, inc_v, w_v, inv_v, coup_v,
+    near_s, near_v, counts_v, nodes_v, up_v, down_v, inc_v, w_v, inv_v, coup_v, inv_t, coup_t,
     picks, onehot, dbuf, dens, snd1, recv1a, recv1b, snd3, recv3, rbuf, wall,
     load_sem, send_sem, recv_sem, ready_sem,
 ):
@@ -120,9 +120,12 @@
         left_half = lax.broadcasted_iota(jnp.int32, block.shape, 2) < cap
         return jnp.where(up_half == left_half, block, pltpu.roll(pltpu.roll(block, modes, 1), cap, 2))
 
-    def inverse_product(k, sides):
+    def inverse_product(k, sides, turned=True):
         first = jnp.concatenate([v for real, imag in sides for v in (real, imag)], 0).astype(BF)
         second = jnp.concatenate([v for real, imag in sides for v in (-imag, real)], 0).astype(BF)
+        if turned:
+            real = jnp.dot(first, inv_t[k, 0], preferred_element_type=F32)
+            return real + jnp.dot(second, inv_t[k, 1], preferred_element_type=F32)
         return dot_nt(first, inv_v[k, 0]) + dot_nt(second, inv_v[k, 1])
 
     def hold(k, h, value):
@@ -162,7 +165,7 @@
         load_inv[k].wait()
         real, imag = inc_v[k, 0].astype(F32), inc_v[k, 1].astype(F32)
         cut = [slice(part * h, part * (h + 1)) for h in range(2)]
-        value = inverse_product(k, [(real[c], imag[c]) for c in cut])
+        value = inverse_product(k, [(real[c], imag[c]) for c in cut], turned=False)
         for h in range(2):
             hold(k, h, value[2 * part * h : 2 * part * (h + 1)])
     for h in range(2):
@@ -199,6 +202,14 @@
     load_down.wait()
     load_coup.wait()
 
+    for c in range(2):
+        coup_t[c] = jnp.transpose(coup_v[c])
+
+    @pl.loop(0, modes)
+    def _(k):
+        for c in range(2):
+            inv_t[k, c] = jnp.transpose(inv_v[k, c])
+
     for it in range(ITERS):
         from_body = (recv1a, recv1b)[it]
         arrived(from_body, it)
@@ -214,7 +225,8 @@
         scaled = jnp.concatenate([cycles[:NA] * weights, cycles[NA:] * weights], 0).astype(BF)
         back = jnp.dot(down_v[...], scaled, preferred_element_type=F32).astype(BF)
         half = back.shape[0] // 2
-        correction = dot_nt(back[:half], coup_v[0]) + dot_nt(back[half:], coup_v[1])
+        correction = jnp.dot(back[:half], coup_t[0], preferred_element_type=F32)
+        correction = correction + jnp.dot(back[half:], coup_t[1], preferred_element_type=F32)
         for j in range(n_mode):
             snd3[it, j] = correction[2 * modes * j : 2 * modes * (j + 1)].astype(BF)
         for off in peers:
@@ -295,6 +307,8 @@
                 pltpu.VMEM((NA // n_mode, slots), BF),
                 pltpu.VMEM((modes, 2, nodes, nodes), BF),
                 pltpu.VMEM((2, nodes, slots), BF),
+                pltpu.VMEM((modes, 2, nodes, nodes), BF),
+                pltpu.VMEM((2, slots, nodes), BF),
                 pltpu.VMEM((bodies, 2 * cap), jnp.int32),
                 pltpu.VMEM((bodies * cap // width, nodes, width), BF),
                 pltpu.VMEM((2, nodes // 128, rows // 2, 128), F32),

time: 44.1 us -> 42.5 us (0.964)
  Pallas kernels: 43.4 us -> 41.7 us
    pallas_call x1, Pallas kernels: 43.4 us -> 41.7 us  [local(): pl.pallas_call(lambda *refs: kernel(n_mode, n_body, *refs), out_shape=plt...]
where the time goes in v4:
time: 42.5 us; the launch traced here: 42.4 us
  Pallas kernels  41.7 us (98%)
  local copies, waits for them, and re-layouts  0.63 us (1%)
    pallas_call x1, Pallas kernels, local(): pl.pallas_call(lambda *refs: kernel(n_mode, n_body, *refs), out_shape=plt...  41.7 us

profile of v4, /device:TPU:1, one launch (start us, length us, event | category | flops | bytes accessed | tf_op | source)
XLA Modules:
  0.0 42.4 jit_solution(2175681691063520349)
XLA Ops:
  0.0 41.7 %sweeps.1 = bf16[64,512]{1,0:T(8,128)(2,1)S(1)} custom-call(s32[6,32]{1,0:T(8,128)} %bitcast.14, s32[6,32]{1,0:T(8,128)} %bitcast.15, s32[6,32,64]{2,1,0:T(8,128)} %bitcast.11, bf16[512,64]{1,0:T(8,128)(2,1)} %constant.4.clone.refs_3_, bf16[128,512]{1,0:T(8,128)(2,1)} %constant.5.clone.refs_4_, bf16[4,2,8,512]{3,2,1,0:T(8,128)(2,1)} %bitcast.12, ...), custom_call_target="tpu_custom_call" | custom-call | tf_op jit(solution)/shard_map/sweeps/pallas_call | solution.py:294
  41.7 0.6 %copy.11 = bf16[1,4,2,8,512]{4,3,2,1,0:T(8,128)(2,1)} copy(bf16[1,4,2,8,512]{4,3,2,1,0:T(8,128)(2,1)S(1)} %bitcast.8) | data formatting | bytes 131072

commit v5 on v4

--- a/solution.py
+++ b/solution.py
@@ -74,6 +74,9 @@
     load_inc, load_near, load_counts, load_nodes = loads[:4]
     load_inv, (load_near_s, load_up, load_down, load_w, load_coup) = loads[4 : 4 + modes], loads[4 + modes :]
 
+    for load in loads:
+        load.start()
+
     barrier = pltpu.get_barrier_semaphore()
     for dy, dz in order[:-1]:
         pl.semaphore_signal(
@@ -83,8 +86,6 @@
         pl.semaphore_signal(
             barrier, inc=1, device_id={"mode": lax.rem(me + off, n_mode)}, device_id_type=MESH
         )
-    for load in loads:
-        load.start()
 
     load_near.wait()
     load_counts.wait()
@@ -103,11 +104,15 @@
     per_group = width // cap
     node_index = lax.broadcasted_iota(jnp.int32, (onehot.shape[1], 2 * cap), 0)
     low = lax.broadcasted_iota(jnp.int32, (1, 2 * cap), 1) < cap
-    for r in range(0, n_body, 2):
-        first, second = (picks[pl.ds(target(body, *order[r + j], ydim), 1), :] for j in range(2))
-        row = jnp.where(low, first, second)
-        lanes = (r % per_group) * cap
-        onehot[r // per_group, :, lanes : lanes + 2 * cap] = jnp.where(node_index == row, 1.0, 0.0).astype(BF)
+    def build(start, stop):
+        for r in range(start, stop, 2):
+            first, second = (picks[pl.ds(target(body, *order[r + j], ydim), 1), :] for j in range(2))
+            row = jnp.where(low, first, second)
+            lanes = (r % per_group) * cap
+            hit = jnp.where(node_index == row, 1.0, 0.0).astype(BF)
+            onehot[r // per_group, :, lanes : lanes + 2 * cap] = hit
+
+    build(0, n_body // 2)
 
     def arrived(dst, slot):
         pltpu.make_async_copy(dst, dst, recv_sem.at[slot]).wait()
@@ -124,8 +129,8 @@
         first = jnp.concatenate([v for real, imag in sides for v in (real, imag)], 0).astype(BF)
         second = jnp.concatenate([v for real, imag in sides for v in (-imag, real)], 0).astype(BF)
         if turned:
-            real = jnp.dot(first, inv_t[k, 0], preferred_element_type=F32)
-            return real + jnp.dot(second, inv_t[k, 1], preferred_element_type=F32)
+            right = inv_t[k].reshape(2 * inv_t.shape[2], -1)
+            return jnp.dot(jnp.concatenate([first, second], 1), right, preferred_element_type=F32)
         return dot_nt(first, inv_v[k, 0]) + dot_nt(second, inv_v[k, 1])
 
     def hold(k, h, value):
@@ -161,8 +166,10 @@
         ).start()
 
     load_inc.wait()
+    for load in load_inv:
+        load.wait()
+    build(n_body // 2, n_body)
     for k in range(modes):
-        load_inv[k].wait()
         real, imag = inc_v[k, 0].astype(F32), inc_v[k, 1].astype(F32)
         cut = [slice(part * h, part * (h + 1)) for h in range(2)]
         value = inverse_product(k, [(real[c], imag[c]) for c in cut], turned=False)
@@ -225,8 +232,9 @@
         scaled = jnp.concatenate([cycles[:NA] * weights, cycles[NA:] * weights], 0).astype(BF)
         back = jnp.dot(down_v[...], scaled, preferred_element_type=F32).astype(BF)
         half = back.shape[0] // 2
-        correction = jnp.dot(back[:half], coup_t[0], preferred_element_type=F32)
-        correction = correction + jnp.dot(back[half:], coup_t[1], preferred_element_type=F32)
+        back = jnp.concatenate([back[:half], back[half:]], 1)
+        right = coup_t[...].reshape(2 * coup_t.shape[1], -1)
+        correction = jnp.dot(back, right, preferred_element_type=F32)
         for j in range(n_mode):
             snd3[it, j] = correction[2 * modes * j : 2 * modes * (j + 1)].astype(BF)
         for off in peers:

time: 42.5 us -> 42.4 us (level)
  no operation moved by 1% of the time
where the time goes in v5:
time: 42.4 us
  Pallas kernels  41.7 us (98%)
  local copies, waits for them, and re-layouts  0.63 us (1%)
    pallas_call x1, Pallas kernels, local(): pl.pallas_call(lambda *refs: kernel(n_mode, n_body, *refs), out_shape=plt...  41.7 us

profile of v5, /device:TPU:1, one launch (start us, length us, event | category | flops | bytes accessed | tf_op | source)
XLA Modules:
  0.0 42.4 jit_solution(17569491847943819139)
XLA Ops:
  0.0 41.7 %sweeps.1 = bf16[64,512]{1,0:T(8,128)(2,1)S(1)} custom-call(s32[6,32]{1,0:T(8,128)} %bitcast.14, s32[6,32]{1,0:T(8,128)} %bitcast.15, s32[6,32,64]{2,1,0:T(8,128)} %bitcast.11, bf16[512,64]{1,0:T(8,128)(2,1)} %constant.4.clone.refs_3_, bf16[128,512]{1,0:T(8,128)(2,1)} %constant.5.clone.refs_4_, bf16[4,2,8,512]{3,2,1,0:T(8,128)(2,1)} %bitcast.12, ...), custom_call_target="tpu_custom_call" | custom-call | tf_op jit(solution)/shard_map/sweeps/pallas_call | solution.py:302
  41.7 0.6 %copy.11 = bf16[1,4,2,8,512]{4,3,2,1,0:T(8,128)(2,1)} copy(bf16[1,4,2,8,512]{4,3,2,1,0:T(8,128)(2,1)S(1)} %bitcast.8) | data formatting | bytes 131072

commit v6 on v5

--- a/solution.py
+++ b/solution.py
@@ -212,7 +212,7 @@
     for c in range(2):
         coup_t[c] = jnp.transpose(coup_v[c])
 
-    @pl.loop(0, modes)
+    @pl.loop(0, modes // 2)
     def _(k):
         for c in range(2):
             inv_t[k, c] = jnp.transpose(inv_v[k, c])
@@ -244,6 +244,12 @@
                 recv_sem=recv_sem.at[2 + 2 * it + core], device_id={"mode": peer}, device_id_type=MESH,
             ).start()
         pltpu.make_async_copy(snd3.at[it, me], recv3.at[it, mine], recv_sem.at[2 + 2 * it + core]).start()
+
+        if it == 0:
+            @pl.loop(modes // 2, modes)
+            def _(k):
+                for c in range(2):
+                    inv_t[k, c] = jnp.transpose(inv_v[k, c])
 
         for h in range(2):
             arrived(recv3.at[it, pl.ds(part * h, part)], 2 + 2 * it + h)

time: 42.4 us -> 42.4 us (level)
  no operation moved by 1% of the time
where the time goes in v6:
time: 42.4 us
  Pallas kernels  41.7 us (98%)
  local copies, waits for them, and re-layouts  0.63 us (1%)
    pallas_call x1, Pallas kernels, local(): pl.pallas_call(lambda *refs: kernel(n_mode, n_body, *refs), out_shape=plt...  41.7 us

profile of v6, /device:TPU:1, one launch (start us, length us, event | category | flops | bytes accessed | tf_op | source)
XLA Modules:
  0.0 42.4 jit_solution(9715621137892696184)
XLA Ops:
  0.0 41.7 %sweeps.1 = bf16[64,512]{1,0:T(8,128)(2,1)S(1)} custom-call(s32[6,32]{1,0:T(8,128)} %bitcast.14, s32[6,32]{1,0:T(8,128)} %bitcast.15, s32[6,32,64]{2,1,0:T(8,128)} %bitcast.11, bf16[512,64]{1,0:T(8,128)(2,1)} %constant.4.clone.refs_3_, bf16[128,512]{1,0:T(8,128)(2,1)} %constant.5.clone.refs_4_, bf16[4,2,8,512]{3,2,1,0:T(8,128)(2,1)} %bitcast.12, ...), custom_call_target="tpu_custom_call" | custom-call | tf_op jit(solution)/shard_map/sweeps/pallas_call | solution.py:308
  41.7 0.6 %copy.11 = bf16[1,4,2,8,512]{4,3,2,1,0:T(8,128)(2,1)} copy(bf16[1,4,2,8,512]{4,3,2,1,0:T(8,128)(2,1)S(1)} %bitcast.8) | data formatting | bytes 131072
